TPU v7x, 128 devices: a whole 4x4x4 slice. The times are simulated.
128 devices in a mesh: shot: 4 (over x_hi, core), gx: 4 (over z), gy: 8 (over x_lo, y).
Axes of the slice: x: 4 (x_hi: 2, x_lo: 2; x = x_hi * 2 + x_lo), y: 4, z: 4, core: 2. Of those that a mesh axis runs over, the one named last changes fastest.
Arguments:
- velocity: bfloat16 [512, 256, 256], P(('shot', 'gx'), 'gy'), may hold values from 0.14941406 to 0.34960938
- epsilon: bfloat16 [512, 256, 256], P(('shot', 'gx'), 'gy'), may hold values from 0.049804688 to 0.29882812
- delta: bfloat16 [512, 256, 256], P(('shot', 'gx'), 'gy'), may hold values from 0.019897461 to 0.14941406
- anchors: int32 [4], replicated, may hold values from 0 to 384
- sources: int32 [4, 3], P('shot'), may hold values from 0 to 255, as said below
- wavelet: float32 [4, 4], P('shot'), may hold values from -8 to 8
- p_now: float32 [4, 128, 256, 256], P('shot', 'gx', 'gy'), may hold values from -6 to 6
- p_prev: float32 [4, 128, 256, 256], P('shot', 'gx', 'gy'), may hold values from -6 to 6
- q_now: float32 [4, 128, 256, 256], P('shot', 'gx', 'gy'), may hold values from -6 to 6
- q_prev: float32 [4, 128, 256, 256], P('shot', 'gx', 'gy'), may hold values from -6 to 6
Outputs:
- p_out: float32 [4, 128, 256, 256], P('shot', 'gx', 'gy')
- q_out: float32 [4, 128, 256, 256], P('shot', 'gx', 'gy')
Inputs may be any that keep to these rules, and one draw needn't show every extreme that they name: `sources`: each source lies inside its aperture: x below 128, y below 256, z below 256; some source lies on the aperture's far end along its longest dimension, and some source has x equal to 0.
All inputs are finite; a program needn't handle non-finite values.
Results may differ from a plain program's by a relative error of at most 0.0003.
Values may be sent and summed in bfloat16 or wider, within the bound.
A program may use at most 128 MiB of HBM per device.

v0:
```python
import jax
import jax.numpy as jnp
from jax import lax
from jax.sharding import PartitionSpec as P

STEPS = 4
STENCIL_WEIGHTS = (-205.0 / 72.0, 8.0 / 5.0, -1.0 / 5.0, 8.0 / 315.0, -1.0 / 560.0)


def with_halo(block, sides, width):
    for axis, dim in sides:
        count = lax.axis_size(axis)
        forward = [(i, i + 1) for i in range(count - 1)]
        backward = [(target, source) for source, target in forward]
        low = lax.ppermute(
            lax.slice_in_dim(block, block.shape[dim] - width, None, axis=dim), axis, forward
        )
        high = lax.ppermute(lax.slice_in_dim(block, 0, width, axis=dim), axis, backward)
        block = jnp.concatenate([low, block, high], axis=dim)
    return block


def shifted_up(values, reach):
    filler = jnp.zeros(values.shape[:-1] + (reach,), values.dtype)
    return jnp.concatenate([values[..., reach:], filler], -1)


def shifted_down(values, reach):
    filler = jnp.zeros(values.shape[:-1] + (reach,), values.dtype)
    return jnp.concatenate([filler, values[..., :-reach]], -1)


def vertical_second(values):
    total = STENCIL_WEIGHTS[0] * values
    for reach in range(1, 5):
        total = total + STENCIL_WEIGHTS[reach] * (
            shifted_up(values, reach) + shifted_down(values, reach)
        )
    return total


def horizontal_second(padded, x_count, y_count):
    x_total = STENCIL_WEIGHTS[0] * padded[4 : 4 + x_count, 4 : 4 + y_count]
    for reach in range(1, 5):
        x_total = x_total + STENCIL_WEIGHTS[reach] * (
            padded[4 + reach : 4 + reach + x_count, 4 : 4 + y_count]
            + padded[4 - reach : 4 - reach + x_count, 4 : 4 + y_count]
        )
    y_total = STENCIL_WEIGHTS[0] * padded[4 : 4 + x_count, 4 : 4 + y_count]
    for reach in range(1, 5):
        y_total = y_total + STENCIL_WEIGHTS[reach] * (
            padded[4 : 4 + x_count, 4 + reach : 4 + reach + y_count]
            + padded[4 : 4 + x_count, 4 - reach : 4 - reach + y_count]
        )
    return x_total + y_total


def update(padded_p, p_field, p_before, q_field, q_before, courant_sq, horiz_gain, cross_gain):
    laplace_h = horizontal_second(padded_p, p_field.shape[0], p_field.shape[1])
    depth_term = vertical_second(q_field)
    p_next = (
        2.0 * p_field - p_before + courant_sq * (horiz_gain * laplace_h + cross_gain * depth_term)
    )
    q_next = 2.0 * q_field - q_before + courant_sq * (cross_gain * laplace_h + depth_term)
    return (p_next, q_next)


def window_rows(pieces, offset, row_count):
    total_rows = pieces.shape[0]
    padded = jnp.pad(pieces, ((row_count, row_count), (0, 0), (0, 0)))
    begin_at = jnp.clip(offset + row_count, 0, total_rows + row_count)
    return lax.dynamic_slice_in_dim(padded, begin_at, row_count, 0)


def source_mask(sources, x_count, y_count, z_count, x_first, y_first):
    x_match = (jnp.arange(x_count, dtype=jnp.int32) + x_first == sources[0, 0]).astype(jnp.float32)
    y_match = (jnp.arange(y_count, dtype=jnp.int32) + y_first == sources[0, 1]).astype(jnp.float32)
    z_match = (jnp.arange(z_count, dtype=jnp.int32) == sources[0, 2]).astype(jnp.float32)
    return x_match[:, None, None] * y_match[None, :, None] * z_match[None, None, :]


def on_device(velocity, epsilon, delta, anchors, sources, wavelet, p_now, p_prev, q_now, q_prev):
    x_cells = p_now.shape[1]
    y_cells = p_now.shape[2]
    z_cells = p_now.shape[3]
    shot_index = lax.axis_index("shot")
    x_index = lax.axis_index("gx")
    y_index = lax.axis_index("gy")
    base_row = anchors[shot_index] + x_index * x_cells
    pieces = (
        lax.all_gather(velocity, ("shot", "gx"), axis=0, tiled=True),
        lax.all_gather(epsilon, ("shot", "gx"), axis=0, tiled=True),
        lax.all_gather(delta, ("shot", "gx"), axis=0, tiled=True),
    )
    velocity_block, epsilon_block, delta_block = tuple(
        (window_rows(piece_one, base_row, x_cells) for piece_one in pieces)
    )
    courant_sq = velocity_block.astype(jnp.float32) * velocity_block.astype(jnp.float32)
    horiz_gain = 1.0 + 2.0 * epsilon_block.astype(jnp.float32)
    cross_gain = jnp.sqrt(1.0 + 2.0 * delta_block.astype(jnp.float32))
    x_first = x_index * x_cells
    y_first = y_index * y_cells
    inner_source = source_mask(sources, x_cells, y_cells, z_cells, x_first, y_first)
    p_field = p_now[0]
    p_before = p_prev[0]
    q_field = q_now[0]
    q_before = q_prev[0]
    for step_index in range(STEPS):
        padded = with_halo(p_field, (("gx", 0), ("gy", 1)), 4)
        p_next, q_next = update(
            padded, p_field, p_before, q_field, q_before, courant_sq, horiz_gain, cross_gain
        )
        p_next = p_next + wavelet[0, step_index] * inner_source
        p_before, p_field, q_before, q_field = (p_field, p_next, q_field, q_next)
    return (p_field[None], q_field[None])


def solution(mesh):
    return jax.shard_map(
        on_device,
        mesh=mesh,
        in_specs=(
            P(("shot", "gx"), "gy", None),
            P(("shot", "gx"), "gy", None),
            P(("shot", "gx"), "gy", None),
            P(),
            P("shot", None),
            P("shot", None),
            P("shot", "gx", "gy", None),
            P("shot", "gx", "gy", None),
            P("shot", "gx", "gy", None),
            P("shot", "gx", "gy", None),
        ),
        out_specs=(P("shot", "gx", "gy", None), P("shot", "gx", "gy", None)),
        check_vma=False,
    )
```

profile of v0, /device:TPU:2, one launch (start us, length us, event | category | flops | bytes accessed | tf_op | source)
XLA Modules:
  0.0 381.0 jit_solution(8481441208767258015)
XLA Ops:
  7.2 0.7 all-gather.4.cloned.1.call-update
  8.0 0.7 all-gather.6.cloned.1.call-update
  8.7 0.7 all-gather.8.cloned.1.call-update
  9.4 3.8 %collective-permute-start.1 = (f32[4,32,256]{2,1,0:T(8,128)S(1)}, f32[4,32,256]{2,1,0:T(8,128)S(1)}, u32[]{:S(2)}, u32[]{:S(2)}) collective-permute-start(f32[4,32,256]{2,1,0:T(8,128)S(1)} %get-tuple-element.68), channel_id=1, source_target_pairs={{0,8},{8,16},{16,24},{1,9},{9,17},{17,25},{2,10},{10,18},{18,26},{... | collective-permute-start | bytes 393224 | tf_op jit(solution)/shard_map/ppermute | solution.py:15
  13.3 1.3 collective-permute-start
  14.6 0.6 fusion.139
  15.2 1.3 compare_convert_fusion.1
  16.5 1.7 fusion.135
  18.2 1.7 fusion.136
  19.9 1.7 fusion.134
  21.6 1.7 fusion.137
  23.3 0.1 broadcast_multiply_fusion
  23.4 4.9 %collective-permute-start.2 = (f32[40,4,256]{2,1,0:T(4,128)S(1)}, f32[40,4,256]{2,1,0:T(4,128)S(1)}, u32[]{:S(2)}, u32[]{:S(2)}) collective-permute-start(f32[40,4,256]{2,1,0:T(4,128)S(1)} %get-tuple-element.28), channel_id=1, source_target_pairs={{1,0},{2,1},{3,2},{4,3},{5,4},{6,5},{7,6},{9,8},{10,9},{11,10},{12... | collective-permute-start | bytes 491528 | tf_op jit(solution)/shard_map/ppermute | solution.py:18
  28.4 1.9 collective-permute-start.3
  30.3 0.6 compare_convert_fusion
  30.9 0.6 dynamic_slice.12
  32.0 0.6 fusion.138
  32.7 0.2 collective-permute-done.2
  32.8 4.9 %collective-permute-done.3 = f32[40,4,256]{2,1,0:T(4,128)S(1)} collective-permute-done((f32[40,4,256]{2,1,0:T(4,128)S(1)}, f32[40,4,256]{2,1,0:T(4,128)S(1)}, u32[]{:S(2)}, u32[]{:S(2)}) %collective-permute-start.3) | collective-permute-done | bytes 163872 | tf_op jit(solution)/shard_map/ppermute | solution.py:15
  37.7 2.0 pad_maximum_fusion
  39.7 45.4 %all-gather.4.cloned.1.call-done = bf16[512,32,256]{2,1,0:T(8,128)(2,1)} async-done(((bf16[32,32,256]{2,1,0:T(8,128)(2,1)}), bf16[512,32,256]{2,1,0:T(8,128)(2,1)}) %all-gather.4.cloned.1.call-update) | async-done | bytes 8388624 | tf_op jit(solution)/shard_map/all_gather | solution.py:91
  85.1 73.3 %all-gather.6.cloned.1.call-done = bf16[512,32,256]{2,1,0:T(8,128)(2,1)} async-done(((bf16[32,32,256]{2,1,0:T(8,128)(2,1)}), bf16[512,32,256]{2,1,0:T(8,128)(2,1)}) %all-gather.6.cloned.1.call-update) | async-done | bytes 8388624 | tf_op jit(solution)/shard_map/all_gather | solution.py:92
  158.5 73.3 %all-gather.8.cloned.1.call-done = bf16[512,32,256]{2,1,0:T(8,128)(2,1)} async-done(((bf16[32,32,256]{2,1,0:T(8,128)(2,1)}), bf16[512,32,256]{2,1,0:T(8,128)(2,1)}) %all-gather.8.cloned.1.call-update) | async-done | bytes 8388624 | tf_op jit(solution)/shard_map/all_gather | solution.py:93
  231.8 12.7 %fusion.68 = (f32[32,32,256]{2,1,0:T(8,128)S(1)}, f32[32,32,256]{2,1,0:T(8,128)S(1)}, f32[32,32,256]{2,1,0:T(8,128)}) fusion(f32[1,32,32,256]{3,2,1,0:T(8,128)} %param.17, f32[256]{0:T(256)S(1)} %compare_convert_fusion, f32[32,32]{1,0:T(8,128)S(1)} %broadcast_multiply_fusion, f32[]{:T(128)} %bitcast.6, f32[1,32,32,256]{3,2,1,0:T(8,128)S(1)} %copy-done.1, ...), kind=kLoop, calls=%fused_computation.131 | loop fusion | flops 17039360 | bytes 49468424 | tf_op jit(solution)/shard_map/add | solution.py:113
  244.6 2.8 fusion.113
  247.3 1.7 fusion.131
  249.0 1.7 fusion.130
  250.8 2.1 collective-permute-start.5
  252.9 1.3 collective-permute-start.4
  254.2 1.7 fusion.132
  255.9 4.1 %collective-permute-done.4 = f32[4,32,256]{2,1,0:T(8,128)S(1)} collective-permute-done((f32[4,32,256]{2,1,0:T(8,128)S(1)}, f32[4,32,256]{2,1,0:T(8,128)S(1)}, u32[]{:S(2)}, u32[]{:S(2)}) %collective-permute-start.4) | collective-permute-done | bytes 131104 | tf_op jit(solution)/shard_map/ppermute | solution.py:18
  260.1 5.5 %collective-permute-start.6 = (f32[40,4,256]{2,1,0:T(4,128)S(1)}, f32[40,4,256]{2,1,0:T(4,128)S(1)}, u32[]{:S(2)}, u32[]{:S(2)}) collective-permute-start(f32[40,4,256]{2,1,0:T(4,128)S(1)} %get-tuple-element.24), channel_id=1, source_target_pairs={{1,0},{2,1},{3,2},{4,3},{5,4},{6,5},{7,6},{9,8},{10,9},{11,10},{12... | collective-permute-start | bytes 491528 | tf_op jit(solution)/shard_map/ppermute | solution.py:18
  265.7 2.1 collective-permute-start.7
  267.8 1.7 fusion.129
  269.4 5.5 %collective-permute-done.7 = f32[40,4,256]{2,1,0:T(4,128)S(1)} collective-permute-done((f32[40,4,256]{2,1,0:T(4,128)S(1)}, f32[40,4,256]{2,1,0:T(4,128)S(1)}, u32[]{:S(2)}, u32[]{:S(2)}) %collective-permute-start.7) | collective-permute-done | bytes 163872 | tf_op jit(solution)/shard_map/ppermute | solution.py:15
  275.0 2.0 pad_maximum_fusion.1
  277.0 12.2 %fusion.69 = (f32[32,32,256]{2,1,0:T(8,128)S(1)}, f32[32,32,256]{2,1,0:T(8,128)}, f32[32,32,256]{2,1,0:T(8,128)}) fusion(f32[32,32,256]{2,1,0:T(8,128)S(1)} %get-tuple-element.11, f32[]{:T(128)} %bitcast.11, f32[256]{0:T(256)S(1)} %compare_convert_fusion, f32[32,32]{1,0:T(8,128)S(1)} %broadcast_multiply_fusion, f32[1,32,32,256]{3,2,1,0:T(8,128)S(1)} %copy-done.1, ...), kind=kLoop, calls=%fused_computation.132 | loop fusion | flops 17039360 | bytes 48419848 | tf_op jit(solution)/shard_map/add | solution.py:113
  289.2 2.4 multiply_add_fusion.3
  291.6 1.7 fusion.126
  293.3 1.7 fusion.125
  295.0 3.1 collective-permute-start.9
  298.2 1.3 collective-permute-start.8
  299.5 1.7 fusion.127
  301.2 3.9 %collective-permute-done.8 = f32[4,32,256]{2,1,0:T(8,128)S(1)} collective-permute-done((f32[4,32,256]{2,1,0:T(8,128)S(1)}, f32[4,32,256]{2,1,0:T(8,128)S(1)}, u32[]{:S(2)}, u32[]{:S(2)}) %collective-permute-start.8) | collective-permute-done | bytes 131104 | tf_op jit(solution)/shard_map/ppermute | solution.py:18
  305.1 1.9 collective-permute-start.10
  307.0 3.9 %collective-permute-start.11 = (f32[40,4,256]{2,1,0:T(4,128)S(1)}, f32[40,4,256]{2,1,0:T(4,128)S(1)}, u32[]{:S(2)}, u32[]{:S(2)}) collective-permute-start(f32[40,4,256]{2,1,0:T(4,128)S(1)} %get-tuple-element.21), channel_id=1, source_target_pairs={{0,1},{1,2},{2,3},{3,4},{4,5},{5,6},{6,7},{8,9},{9,10},{10,11},{11... | collective-permute-start | bytes 491528 | tf_op jit(solution)/shard_map/ppermute | solution.py:15
  311.0 1.7 fusion.124
  312.6 3.7 collective-permute-done.11
  316.4 2.0 pad_maximum_fusion.2
  318.3 12.2 %fusion.70 = (f32[32,32,256]{2,1,0:T(8,128)S(1)}, f32[32,32,256]{2,1,0:T(8,128)}, f32[32,32,256]{2,1,0:T(8,128)}) fusion(f32[32,32,256]{2,1,0:T(8,128)S(1)} %copy-done.3, f32[32,32,256]{2,1,0:T(8,128)S(1)} %get-tuple-element.8, f32[]{:T(128)} %bitcast.12, f32[256]{0:T(256)S(1)} %compare_convert_fusion, f32[32,32]{1,0:T(8,128)S(1)} %broadcast_multiply_fusion, ...), kind=kLoop, calls=%fused_computation.133 | loop fusion | flops 17039360 | bytes 48419848 | tf_op jit(solution)/shard_map/add | solution.py:113
  330.5 2.4 multiply_add_fusion.1
  333.0 1.7 fusion.122
  334.7 1.8 fusion.120
  336.4 2.9 collective-permute-start.13
  339.4 1.3 collective-permute-start.12
  340.7 1.7 fusion.121
  342.4 3.8 %collective-permute-done.12 = f32[4,32,256]{2,1,0:T(8,128)S(1)} collective-permute-done((f32[4,32,256]{2,1,0:T(8,128)S(1)}, f32[4,32,256]{2,1,0:T(8,128)S(1)}, u32[]{:S(2)}, u32[]{:S(2)}) %collective-permute-start.12) | collective-permute-done | bytes 131104 | tf_op jit(solution)/shard_map/ppermute | solution.py:18
  346.3 1.9 collective-permute-start.14
  348.2 4.1 %collective-permute-start.15 = (f32[40,4,256]{2,1,0:T(4,128)S(1)}, f32[40,4,256]{2,1,0:T(4,128)S(1)}, u32[]{:S(2)}, u32[]{:S(2)}) collective-permute-start(f32[40,4,256]{2,1,0:T(4,128)S(1)} %get-tuple-element.17), channel_id=1, source_target_pairs={{0,1},{1,2},{2,3},{3,4},{4,5},{5,6},{6,7},{8,9},{9,10},{10,11},{11... | collective-permute-start | bytes 491528 | tf_op jit(solution)/shard_map/ppermute | solution.py:15
  352.4 1.7 fusion.119
  354.1 3.5 collective-permute-done.15
  357.6 2.0 pad_maximum_fusion.3
  359.5 10.9 %add_bitcast_fusion = (f32[1,32,32,256]{3,2,1,0:T(8,128)}, f32[32,32,256]{2,1,0:T(8,128)S(1)}, f32[32,32,256]{2,1,0:T(8,128)}) fusion(f32[32,32,256]{2,1,0:T(8,128)S(1)} %multiply_add_fusion.3, f32[32,32,256]{2,1,0:T(8,128)S(1)} %multiply_add_fusion.1, s32[]{:T(128)S(6)} %min.6, bf16[512,32,256]{2,1,0:T(8,128)(2,1)S(1)} %bitcast.35, ...), kind=kLoop, calls=%fused_computation.204 | loop fusion | flops 15204352 | bytes 40026116 | tf_op jit(solution)/shard_map/broadcast_in_dim | solution.py:115
  370.5 4.0 %fusion.72 = f32[1,32,32,256]{3,2,1,0:T(8,128)} fusion(f32[32,32,256]{2,1,0:T(8,128)} %get-tuple-element.4, f32[32,32,256]{2,1,0:T(8,128)S(1)} %get-tuple-element.3, f32[32,32,256]{2,1,0:T(8,128)S(1)} %get-tuple-element.8, f32[32,32,256]{2,1,0:T(8,128)S(1)} %get-tuple-element.5, f32[]{:T(128)} %bitcast.13, f32[256]{0:T(256)S(1)} %compare_convert_fusion, ...), kind=kLoop, calls=%fused_computation.135 | loop fusion | flops 4718592 | bytes 30413832 | tf_op jit(solution)/shard_map/broadcast_in_dim | solution.py:115
  (38 shorter events, 0.5 us)
Async XLA Ops:
  7.2 2.3 copy-start.1
  7.2 7.4 %copy-start.5 = (s32[1,3]{1,0:T(1,128)S(1)}, s32[1,3]{1,0:T(1,128)}, u32[]{:S(2)}) copy-start(s32[1,3]{1,0:T(1,128)} %param.14) | copy-start | bytes 40
  7.2 9.3 %copy-start = (f32[1,32,32,256]{3,2,1,0:T(8,128)S(1)}, f32[1,32,32,256]{3,2,1,0:T(8,128)}, u32[]{:S(2)}) copy-start(f32[1,32,32,256]{3,2,1,0:T(8,128)} %param.18) | copy-start | bytes 3145732
  7.2 77.9 %all-gather.4.cloned.1.call-start = ((), (), s32[]{:S(2)}) async-start(), calls=%async_computation | async-start | bytes 8912896 | tf_op jit(solution)/shard_map/all_gather | solution.py:91
  7.9 150.5 %all-gather.6.cloned.1.call-start = ((), (), s32[]{:S(2)}) async-start(), calls=%async_computation.1 | async-start | bytes 8912896 | tf_op jit(solution)/shard_map/all_gather | solution.py:92
  8.7 223.1 %all-gather.8.cloned.1.call-start = ((), (), s32[]{:S(2)}) async-start(), calls=%async_computation.2 | async-start | bytes 8912896 | tf_op jit(solution)/shard_map/all_gather | solution.py:93
  9.4 13.9 %collective-permute-start.1 = (f32[4,32,256]{2,1,0:T(8,128)S(1)}, f32[4,32,256]{2,1,0:T(8,128)S(1)}, u32[]{:S(2)}, u32[]{:S(2)}) collective-permute-start(f32[4,32,256]{2,1,0:T(8,128)S(1)} %get-tuple-element.68), channel_id=1, source_target_pairs={{0,8},{8,16},{16,24},{1,9},{9,17},{17,25},{2,10},{10,18},{18,26},{... | collective-permute-start | bytes 393224 | tf_op jit(solution)/shard_map/ppermute | solution.py:15
  13.3 10.1 %collective-permute-start = (f32[4,32,256]{2,1,0:T(8,128)S(1)}, f32[4,32,256]{2,1,0:T(8,128)S(1)}, u32[]{:S(2)}, u32[]{:S(2)}) collective-permute-start(f32[4,32,256]{2,1,0:T(8,128)S(1)} %get-tuple-element.69), channel_id=1, source_target_pairs={{8,0},{16,8},{24,16},{9,1},{17,9},{25,17},{10,2},{18,10},{26,18},{... | collective-permute-start | bytes 393224 | tf_op jit(solution)/shard_map/ppermute | solution.py:18
  23.3 7.6 %copy-start.6 = (s32[4]{0:T(128)S(1)}, s32[4]{0:T(128)}, u32[]{:S(2)}) copy-start(s32[4]{0:T(128)} %param.13) | copy-start | bytes 52
  23.3 8.7 %copy-start.4 = (f32[1,4]{1,0:T(1,128)S(1)}, f32[1,4]{1,0:T(1,128)}, u32[]{:S(2)}) copy-start(f32[1,4]{1,0:T(1,128)} %param.15) | copy-start | bytes 52
  23.4 9.4 %collective-permute-start.2 = (f32[40,4,256]{2,1,0:T(4,128)S(1)}, f32[40,4,256]{2,1,0:T(4,128)S(1)}, u32[]{:S(2)}, u32[]{:S(2)}) collective-permute-start(f32[40,4,256]{2,1,0:T(4,128)S(1)} %get-tuple-element.28), channel_id=1, source_target_pairs={{1,0},{2,1},{3,2},{4,3},{5,4},{6,5},{7,6},{9,8},{10,9},{11,10},{12... | collective-permute-start | bytes 491528 | tf_op jit(solution)/shard_map/ppermute | solution.py:18
  28.4 9.4 %collective-permute-start.3 = (f32[40,4,256]{2,1,0:T(4,128)S(1)}, f32[40,4,256]{2,1,0:T(4,128)S(1)}, u32[]{:S(2)}, u32[]{:S(2)}) collective-permute-start(f32[40,4,256]{2,1,0:T(4,128)S(1)} %get-tuple-element.29), channel_id=1, source_target_pairs={{0,1},{1,2},{2,3},{3,4},{4,5},{5,6},{6,7},{8,9},{9,10},{10,11},{11... | collective-permute-start | bytes 491528 | tf_op jit(solution)/shard_map/ppermute | solution.py:15
  231.8 12.7 %slice-start = ((s8[8388608]{0:T(1024)(128)(4,1)}), s8[4194304]{0:T(1024)(128)(4,1)S(1)}, s32[]{:S(2)}) async-start(s8[8388608]{0:T(1024)(128)(4,1)} %bitcast.34), calls=%async_computation.3 | async-start | bytes 8388608
  231.8 12.7 %slice-start.1 = ((s8[8388608]{0:T(1024)(128)(4,1)}), s8[4194304]{0:T(1024)(128)(4,1)S(1)}, s32[]{:S(2)}) async-start(s8[8388608]{0:T(1024)(128)(4,1)} %bitcast.34), calls=%async_computation.4 | async-start | bytes 8388608
  244.5 32.4 %copy-start.2 = (f32[32,32,256]{2,1,0:T(8,128)}, f32[32,32,256]{2,1,0:T(8,128)S(1)}, u32[]{:S(2)}) copy-start(f32[32,32,256]{2,1,0:T(8,128)S(1)} %get-tuple-element.11) | copy-start | bytes 3145732
  250.8 5.1 %collective-permute-start.5 = (f32[4,32,256]{2,1,0:T(8,128)S(1)}, f32[4,32,256]{2,1,0:T(8,128)S(1)}, u32[]{:S(2)}, u32[]{:S(2)}) collective-permute-start(f32[4,32,256]{2,1,0:T(8,128)S(1)} %get-tuple-element.58), channel_id=1, source_target_pairs={{0,8},{8,16},{16,24},{1,9},{9,17},{17,25},{2,10},{10,18},{18,26},{... | collective-permute-start | bytes 393224 | tf_op jit(solution)/shard_map/ppermute | solution.py:15
  252.9 7.2 %collective-permute-start.4 = (f32[4,32,256]{2,1,0:T(8,128)S(1)}, f32[4,32,256]{2,1,0:T(8,128)S(1)}, u32[]{:S(2)}, u32[]{:S(2)}) collective-permute-start(f32[4,32,256]{2,1,0:T(8,128)S(1)} %get-tuple-element.59), channel_id=1, source_target_pairs={{8,0},{16,8},{24,16},{9,1},{17,9},{25,17},{10,2},{18,10},{26,18},{... | collective-permute-start | bytes 393224 | tf_op jit(solution)/shard_map/ppermute | solution.py:18
  260.1 9.3 %collective-permute-start.6 = (f32[40,4,256]{2,1,0:T(4,128)S(1)}, f32[40,4,256]{2,1,0:T(4,128)S(1)}, u32[]{:S(2)}, u32[]{:S(2)}) collective-permute-start(f32[40,4,256]{2,1,0:T(4,128)S(1)} %get-tuple-element.24), channel_id=1, source_target_pairs={{1,0},{2,1},{3,2},{4,3},{5,4},{6,5},{7,6},{9,8},{10,9},{11,10},{12... | collective-permute-start | bytes 491528 | tf_op jit(solution)/shard_map/ppermute | solution.py:18
  265.7 9.3 %collective-permute-start.7 = (f32[40,4,256]{2,1,0:T(4,128)S(1)}, f32[40,4,256]{2,1,0:T(4,128)S(1)}, u32[]{:S(2)}, u32[]{:S(2)}) collective-permute-start(f32[40,4,256]{2,1,0:T(4,128)S(1)} %get-tuple-element.25), channel_id=1, source_target_pairs={{0,1},{1,2},{2,3},{3,4},{4,5},{5,6},{6,7},{8,9},{9,10},{10,11},{11... | collective-permute-start | bytes 491528 | tf_op jit(solution)/shard_map/ppermute | solution.py:15
  295.0 6.1 %collective-permute-start.9 = (f32[4,32,256]{2,1,0:T(8,128)S(1)}, f32[4,32,256]{2,1,0:T(8,128)S(1)}, u32[]{:S(2)}, u32[]{:S(2)}) collective-permute-start(f32[4,32,256]{2,1,0:T(8,128)S(1)} %get-tuple-element.48), channel_id=1, source_target_pairs={{0,8},{8,16},{16,24},{1,9},{9,17},{17,25},{2,10},{10,18},{18,26},{... | collective-permute-start | bytes 393224 | tf_op jit(solution)/shard_map/ppermute | solution.py:15
  298.2 6.9 %collective-permute-start.8 = (f32[4,32,256]{2,1,0:T(8,128)S(1)}, f32[4,32,256]{2,1,0:T(8,128)S(1)}, u32[]{:S(2)}, u32[]{:S(2)}) collective-permute-start(f32[4,32,256]{2,1,0:T(8,128)S(1)} %get-tuple-element.49), channel_id=1, source_target_pairs={{8,0},{16,8},{24,16},{9,1},{17,9},{25,17},{10,2},{18,10},{26,18},{... | collective-permute-start | bytes 393224 | tf_op jit(solution)/shard_map/ppermute | solution.py:18
  305.1 7.5 %collective-permute-start.10 = (f32[40,4,256]{2,1,0:T(4,128)S(1)}, f32[40,4,256]{2,1,0:T(4,128)S(1)}, u32[]{:S(2)}, u32[]{:S(2)}) collective-permute-start(f32[40,4,256]{2,1,0:T(4,128)S(1)} %get-tuple-element.20), channel_id=1, source_target_pairs={{1,0},{2,1},{3,2},{4,3},{5,4},{6,5},{7,6},{9,8},{10,9},{11,10},{12... | collective-permute-start | bytes 491528 | tf_op jit(solution)/shard_map/ppermute | solution.py:18
  307.0 9.3 %collective-permute-start.11 = (f32[40,4,256]{2,1,0:T(4,128)S(1)}, f32[40,4,256]{2,1,0:T(4,128)S(1)}, u32[]{:S(2)}, u32[]{:S(2)}) collective-permute-start(f32[40,4,256]{2,1,0:T(4,128)S(1)} %get-tuple-element.21), channel_id=1, source_target_pairs={{0,1},{1,2},{2,3},{3,4},{4,5},{5,6},{6,7},{8,9},{9,10},{10,11},{11... | collective-permute-start | bytes 491528 | tf_op jit(solution)/shard_map/ppermute | solution.py:15
  312.6 5.7 %copy-start.3 = (f32[32,32,256]{2,1,0:T(8,128)S(1)}, f32[32,32,256]{2,1,0:T(8,128)}, u32[]{:S(2)}) copy-start(f32[32,32,256]{2,1,0:T(8,128)} %copy-done.2) | copy-start | bytes 3145732
  336.4 6.0 %collective-permute-start.13 = (f32[4,32,256]{2,1,0:T(8,128)S(1)}, f32[4,32,256]{2,1,0:T(8,128)S(1)}, u32[]{:S(2)}, u32[]{:S(2)}) collective-permute-start(f32[4,32,256]{2,1,0:T(8,128)S(1)} %get-tuple-element.38), channel_id=1, source_target_pairs={{0,8},{8,16},{16,24},{1,9},{9,17},{17,25},{2,10},{10,18},{18,26},{... | collective-permute-start | bytes 393224 | tf_op jit(solution)/shard_map/ppermute | solution.py:15
  339.4 6.9 %collective-permute-start.12 = (f32[4,32,256]{2,1,0:T(8,128)S(1)}, f32[4,32,256]{2,1,0:T(8,128)S(1)}, u32[]{:S(2)}, u32[]{:S(2)}) collective-permute-start(f32[4,32,256]{2,1,0:T(8,128)S(1)} %get-tuple-element.39), channel_id=1, source_target_pairs={{8,0},{16,8},{24,16},{9,1},{17,9},{25,17},{10,2},{18,10},{26,18},{... | collective-permute-start | bytes 393224 | tf_op jit(solution)/shard_map/ppermute | solution.py:18
  346.3 7.8 %collective-permute-start.14 = (f32[40,4,256]{2,1,0:T(4,128)S(1)}, f32[40,4,256]{2,1,0:T(4,128)S(1)}, u32[]{:S(2)}, u32[]{:S(2)}) collective-permute-start(f32[40,4,256]{2,1,0:T(4,128)S(1)} %get-tuple-element.16), channel_id=1, source_target_pairs={{1,0},{2,1},{3,2},{4,3},{5,4},{6,5},{7,6},{9,8},{10,9},{11,10},{12... | collective-permute-start | bytes 491528 | tf_op jit(solution)/shard_map/ppermute | solution.py:18
  348.2 9.3 %collective-permute-start.15 = (f32[40,4,256]{2,1,0:T(4,128)S(1)}, f32[40,4,256]{2,1,0:T(4,128)S(1)}, u32[]{:S(2)}, u32[]{:S(2)}) collective-permute-start(f32[40,4,256]{2,1,0:T(4,128)S(1)} %get-tuple-element.17), channel_id=1, source_target_pairs={{0,1},{1,2},{2,3},{3,4},{4,5},{5,6},{6,7},{8,9},{9,10},{10,11},{11... | collective-permute-start | bytes 491528 | tf_op jit(solution)/shard_map/ppermute | solution.py:15
Sparse Core Ops, SparseCore 0:
  10.5 74.5 all-gather.3
  87.6 70.8 all-gather.5
  160.9 70.8 all-gather.7
where the time goes:
time: 382 us; the launch traced here: 381 us
  waiting for transfers between devices  224 us (59%)
  other arithmetic  69.8 us (18%)
  starting transfers between devices  43.6 us (11%)
  local copies, waits for them, and re-layouts  29.1 us (8%)
  between operations  14.7 us (4%)
    all_gather x1, waiting for transfers between devices, on_device(): lax.all_gather(delta, ('shot', 'gx'), axis=0, tiled=True)  73.3 us
    all_gather x1, waiting for transfers between devices, on_device(): lax.all_gather(epsilon, ('shot', 'gx'), axis=0, tiled=True)  73.3 us
    all_gather x1, waiting for transfers between devices, on_device(): lax.all_gather(velocity, ('shot', 'gx'), axis=0, tiled=True)  45.4 us
    add x3, other arithmetic, on_device(): p_next = p_next + wavelet[0, step_index] * inner_source  37.1 us
    slice x16, local copies, waits for them, and re-layouts, shifted_up(): return jnp.concatenate([values[..., reach:], filler], -1)  27.2 us
    ppermute x8, starting transfers between devices, with_halo(): lax.ppermute(lax.slice_in_dim(block, block.shape[dim] - width, None, axis...  24.1 us
    ppermute x8, starting transfers between devices, with_halo(): lax.ppermute(lax.slice_in_dim(block, 0, width, axis=dim), axis, backward)  19.5 us
    ppermute x8, waiting for transfers between devices, with_halo(): lax.ppermute(lax.slice_in_dim(block, block.shape[dim] - width, None, axis...  17.7 us
  transfers between devices with their start and end apart: 19, of which 12 were waited for; matrix products, arithmetic and copies ran while one was open for 6% of the time, Pallas kernels for 0%

commit v1 on v0

--- a/solution.py
+++ b/solution.py
@@ -1,3 +1,4 @@
+import functools
 import jax
 import jax.numpy as jnp
 from jax import lax
@@ -5,6 +6,19 @@
 
 STEPS = 4
 STENCIL_WEIGHTS = (-205.0 / 72.0, 8.0 / 5.0, -1.0 / 5.0, 8.0 / 315.0, -1.0 / 560.0)
+
+
+def follow_the_things(panel, axis_name):
+    by_place = []
+    for _ in range(lax.psum(1, axis_name=axis_name)):
+        by_place.append(panel)
+    return jnp.concatenate(
+        lax.all_to_all(jnp.stack(by_place), axis_name=axis_name, split_axis=0, concat_axis=0),
+        axis=0,
+    )
+
+
+_tell_domain = functools.partial(follow_the_things, axis_name=("shot", "gx"))
 
 
 def with_halo(block, sides, width):
@@ -89,7 +103,7 @@
     base_row = anchors[shot_index] + x_index * x_cells
     pieces = (
         lax.all_gather(velocity, ("shot", "gx"), axis=0, tiled=True),
-        lax.all_gather(epsilon, ("shot", "gx"), axis=0, tiled=True),
+        _tell_domain(epsilon),
         lax.all_gather(delta, ("shot", "gx"), axis=0, tiled=True),
     )
     velocity_block, epsilon_block, delta_block = tuple(

time: 382 us -> 378 us (0.990)
  waiting for transfers between devices: 224 us -> 199 us
  starting transfers between devices: 43.6 us -> 58.8 us
  local copies, waits for them, and re-layouts: 29.1 us -> 34.4 us
    ppermute x8, waiting for transfers between devices: 12 us -> 99.5 us  [with_halo(): lax.ppermute(lax.slice_in_dim(block, 0, width, axis=dim), axis, backward)]
    all_gather x1 -> x0, waiting for transfers between devices: 73.3 us -> none  [on_device(): lax.all_gather(epsilon, ('shot', 'gx'), axis=0, tiled=True)]
    all_gather x1, waiting for transfers between devices: 45.4 us -> 5.47 us  [on_device(): lax.all_gather(velocity, ('shot', 'gx'), axis=0, tiled=True)]
    all_to_all x0 -> x1, starting transfers between devices: none -> 7.16 us  [follow_the_things(): lax.all_to_all(jnp.stack(by_place), axis_name=axis_name, split_axis=0, co...]
    ppermute x8, starting transfers between devices: 24.1 us -> 31.1 us  [with_halo(): lax.ppermute(lax.slice_in_dim(block, block.shape[dim] - width, None, axis...]
    another operation x0 -> x1, local copies, waits for them, and re-layouts: none -> 5.37 us  [follow_the_things(): jnp.stack(by_place)]
  transfers between devices with their start and end apart: 19 -> 19, of which waited for: 12 -> 10; matrix products, arithmetic and copies ran while one was open for 6% -> 8% of each run, Pallas kernels for 0% -> 0%
where the time goes in v1:
time: 378 us; the launch traced here: 377 us
  waiting for transfers between devices  199 us (53%)
  other arithmetic  69.1 us (18%)
  starting transfers between devices  58.8 us (16%)
  local copies, waits for them, and re-layouts  34.4 us (9%)
  between operations  14.9 us (4%)
    ppermute x8, waiting for transfers between devices, with_halo(): lax.ppermute(lax.slice_in_dim(block, 0, width, axis=dim), axis, backward)  99.5 us
    all_gather x1, waiting for transfers between devices, on_device(): lax.all_gather(delta, ('shot', 'gx'), axis=0, tiled=True)  72.4 us
    add x3, other arithmetic, on_device(): p_next = p_next + wavelet[0, step_index] * inner_source  36.5 us
    ppermute x8, starting transfers between devices, with_halo(): lax.ppermute(lax.slice_in_dim(block, block.shape[dim] - width, None, axis...  31.1 us
    slice x16, local copies, waits for them, and re-layouts, shifted_up(): return jnp.concatenate([values[..., reach:], filler], -1)  27.1 us
    ppermute x8, waiting for transfers between devices, with_halo(): lax.ppermute(lax.slice_in_dim(block, block.shape[dim] - width, None, axis...  20.5 us
    ppermute x8, starting transfers between devices, with_halo(): lax.ppermute(lax.slice_in_dim(block, 0, width, axis=dim), axis, backward)  20.4 us
    broadcast_in_dim x2, other arithmetic, on_device(): return (p_field[None], q_field[None])  14.8 us
  transfers between devices with their start and end apart: 19, of which 10 were waited for; matrix products, arithmetic and copies ran while one was open for 8% of the time, Pallas kernels for 0%

profile of v1, /device:TPU:2, one launch (start us, length us, event | category | flops | bytes accessed | tf_op | source)
XLA Modules:
  0.0 376.6 jit_solution(1482601684562696576)
XLA Ops:
  7.2 0.7 all-gather.3.cloned.1.call-update
  7.9 0.7 all-gather.5.cloned.1.call-update
  8.6 5.4 %stack.2 = bf16[16,32,32,256]{3,2,1,0:T(8,128)(2,1)} broadcast(bf16[32,32,256]{2,1,0:T(8,128)(2,1)} %param.11), dimensions={1,2,3} | broadcast | bytes 8912896 | tf_op jit(solution)/shard_map/stack | solution.py:16
  14.0 7.2 %all-to-all-start = ((bf16[16,32,32,256]{3,2,1,0:T(8,128)(2,1)}), bf16[16,32,32,256]{3,2,1,0:T(8,128)(2,1)}, u32[]{:S(2)}, u32[]{:S(2)}) async-start(bf16[16,32,32,256]{3,2,1,0:T(8,128)(2,1)} %stack.2), calls=%async_computation | async-start | bytes 16777216 | tf_op jit(solution)/shard_map/all_to_all | solution.py:16
  21.2 1.3 collective-permute-start
  22.5 4.6 %collective-permute-start.1 = (f32[4,32,256]{2,1,0:T(8,128)S(1)}, f32[4,32,256]{2,1,0:T(8,128)S(1)}, u32[]{:S(2)}, u32[]{:S(2)}) collective-permute-start(f32[4,32,256]{2,1,0:T(8,128)S(1)} %get-tuple-element.68), channel_id=1, source_target_pairs={{0,8},{8,16},{16,24},{1,9},{9,17},{17,25},{2,10},{10,18},{18,26},{... | collective-permute-start | bytes 393224 | tf_op jit(solution)/shard_map/ppermute | solution.py:29
  27.1 0.6 fusion.139
  27.7 1.3 compare_convert_fusion.1
  29.0 1.7 fusion.137
  30.7 1.7 fusion.136
  32.4 1.7 fusion.135
  34.1 1.7 fusion.134
  35.8 0.1 broadcast_multiply_fusion
  35.9 99.5 %collective-permute-done = f32[4,32,256]{2,1,0:T(8,128)S(1)} collective-permute-done((f32[4,32,256]{2,1,0:T(8,128)S(1)}, f32[4,32,256]{2,1,0:T(8,128)S(1)}, u32[]{:S(2)}, u32[]{:S(2)}) %collective-permute-start) | collective-permute-done | bytes 131104 | tf_op jit(solution)/shard_map/ppermute | solution.py:32
  135.4 5.9 %collective-permute-start.2 = (f32[40,4,256]{2,1,0:T(4,128)S(1)}, f32[40,4,256]{2,1,0:T(4,128)S(1)}, u32[]{:S(2)}, u32[]{:S(2)}) collective-permute-start(f32[40,4,256]{2,1,0:T(4,128)S(1)} %get-tuple-element.28), channel_id=1, source_target_pairs={{1,0},{2,1},{3,2},{4,3},{5,4},{6,5},{7,6},{9,8},{10,9},{11,10},{12... | collective-permute-start | bytes 491528 | tf_op jit(solution)/shard_map/ppermute | solution.py:32
  141.3 1.9 collective-permute-start.3
  143.2 0.6 compare_convert_fusion
  143.8 0.6 dynamic_slice.12
  145.0 0.7 fusion.138
  145.7 5.2 %collective-permute-done.3 = f32[40,4,256]{2,1,0:T(4,128)S(1)} collective-permute-done((f32[40,4,256]{2,1,0:T(4,128)S(1)}, f32[40,4,256]{2,1,0:T(4,128)S(1)}, u32[]{:S(2)}, u32[]{:S(2)}) %collective-permute-start.3) | collective-permute-done | bytes 163872 | tf_op jit(solution)/shard_map/ppermute | solution.py:29
  150.9 2.1 pad_maximum_fusion
  153.0 5.5 %all-gather.3.cloned.1.call-done = bf16[512,32,256]{2,1,0:T(8,128)(2,1)} async-done(((bf16[32,32,256]{2,1,0:T(8,128)(2,1)}), bf16[512,32,256]{2,1,0:T(8,128)(2,1)}) %all-gather.3.cloned.1.call-update) | async-done | bytes 8388624 | tf_op jit(solution)/shard_map/all_gather | solution.py:105
  158.5 72.4 %all-gather.5.cloned.1.call-done = bf16[512,32,256]{2,1,0:T(8,128)(2,1)} async-done(((bf16[32,32,256]{2,1,0:T(8,128)(2,1)}), bf16[512,32,256]{2,1,0:T(8,128)(2,1)}) %all-gather.5.cloned.1.call-update) | async-done | bytes 8388624 | tf_op jit(solution)/shard_map/all_gather | solution.py:107
  230.9 12.5 %fusion.68 = (f32[32,32,256]{2,1,0:T(8,128)S(1)}, f32[32,32,256]{2,1,0:T(8,128)S(1)}, f32[32,32,256]{2,1,0:T(8,128)}) fusion(f32[1,32,32,256]{3,2,1,0:T(8,128)} %param.17, f32[256]{0:T(256)S(1)} %compare_convert_fusion, f32[32,32]{1,0:T(8,128)S(1)} %broadcast_multiply_fusion, f32[]{:T(128)} %bitcast.7, f32[1,32,32,256]{3,2,1,0:T(8,128)S(1)} %copy-done.1, ...), kind=kLoop, calls=%fused_computation.131 | loop fusion | flops 17039360 | bytes 49468424 | tf_op jit(solution)/shard_map/add | solution.py:127
  243.4 2.8 fusion.113
  246.2 1.7 fusion.132
  247.9 1.7 fusion.131
  249.6 1.3 collective-permute-start.4
  250.9 4.6 %collective-permute-start.5 = (f32[4,32,256]{2,1,0:T(8,128)S(1)}, f32[4,32,256]{2,1,0:T(8,128)S(1)}, u32[]{:S(2)}, u32[]{:S(2)}) collective-permute-start(f32[4,32,256]{2,1,0:T(8,128)S(1)} %get-tuple-element.58), channel_id=1, source_target_pairs={{0,8},{8,16},{16,24},{1,9},{9,17},{17,25},{2,10},{10,18},{18,26},{... | collective-permute-start | bytes 393224 | tf_op jit(solution)/shard_map/ppermute | solution.py:29
  255.4 1.7 fusion.130
  257.2 1.0 collective-permute-done.5
  258.3 5.5 %collective-permute-start.6 = (f32[40,4,256]{2,1,0:T(4,128)S(1)}, f32[40,4,256]{2,1,0:T(4,128)S(1)}, u32[]{:S(2)}, u32[]{:S(2)}) collective-permute-start(f32[40,4,256]{2,1,0:T(4,128)S(1)} %get-tuple-element.24), channel_id=1, source_target_pairs={{1,0},{2,1},{3,2},{4,3},{5,4},{6,5},{7,6},{9,8},{10,9},{11,10},{12... | collective-permute-start | bytes 491528 | tf_op jit(solution)/shard_map/ppermute | solution.py:32
  263.9 2.1 collective-permute-start.7
  266.0 1.7 fusion.129
  267.6 5.6 %collective-permute-done.7 = f32[40,4,256]{2,1,0:T(4,128)S(1)} collective-permute-done((f32[40,4,256]{2,1,0:T(4,128)S(1)}, f32[40,4,256]{2,1,0:T(4,128)S(1)}, u32[]{:S(2)}, u32[]{:S(2)}) %collective-permute-start.7) | collective-permute-done | bytes 163872 | tf_op jit(solution)/shard_map/ppermute | solution.py:29
  273.2 2.0 pad_maximum_fusion.1
  275.1 12.0 %fusion.69 = (f32[32,32,256]{2,1,0:T(8,128)S(1)}, f32[32,32,256]{2,1,0:T(8,128)}, f32[32,32,256]{2,1,0:T(8,128)}) fusion(f32[32,32,256]{2,1,0:T(8,128)S(1)} %get-tuple-element.11, f32[]{:T(128)} %bitcast.12, f32[256]{0:T(256)S(1)} %compare_convert_fusion, f32[32,32]{1,0:T(8,128)S(1)} %broadcast_multiply_fusion, f32[1,32,32,256]{3,2,1,0:T(8,128)S(1)} %copy-done.1, ...), kind=kLoop, calls=%fused_computation.132 | loop fusion | flops 17039360 | bytes 48419848 | tf_op jit(solution)/shard_map/add | solution.py:127
  287.2 2.4 multiply_add_fusion.3
  289.6 1.7 fusion.127
  291.3 1.7 fusion.126
  293.0 1.3 collective-permute-start.8
  294.3 5.0 %collective-permute-start.9 = (f32[4,32,256]{2,1,0:T(8,128)S(1)}, f32[4,32,256]{2,1,0:T(8,128)S(1)}, u32[]{:S(2)}, u32[]{:S(2)}) collective-permute-start(f32[4,32,256]{2,1,0:T(8,128)S(1)} %get-tuple-element.48), channel_id=1, source_target_pairs={{0,8},{8,16},{16,24},{1,9},{9,17},{17,25},{2,10},{10,18},{18,26},{... | collective-permute-start | bytes 393224 | tf_op jit(solution)/shard_map/ppermute | solution.py:29
  299.3 1.7 fusion.125
  301.0 0.8 collective-permute-done.9
  301.8 1.9 collective-permute-start.10
  303.7 3.9 %collective-permute-start.11 = (f32[40,4,256]{2,1,0:T(4,128)S(1)}, f32[40,4,256]{2,1,0:T(4,128)S(1)}, u32[]{:S(2)}, u32[]{:S(2)}) collective-permute-start(f32[40,4,256]{2,1,0:T(4,128)S(1)} %get-tuple-element.21), channel_id=1, source_target_pairs={{0,1},{1,2},{2,3},{3,4},{4,5},{5,6},{6,7},{8,9},{9,10},{10,11},{11... | collective-permute-start | bytes 491528 | tf_op jit(solution)/shard_map/ppermute | solution.py:29
  307.7 1.6 fusion.124
  309.3 3.7 collective-permute-done.11
  313.1 2.0 pad_maximum_fusion.2
  315.0 12.0 %fusion.70 = (f32[32,32,256]{2,1,0:T(8,128)S(1)}, f32[32,32,256]{2,1,0:T(8,128)}, f32[32,32,256]{2,1,0:T(8,128)}) fusion(f32[32,32,256]{2,1,0:T(8,128)S(1)} %copy-done.3, f32[32,32,256]{2,1,0:T(8,128)S(1)} %get-tuple-element.8, f32[]{:T(128)} %bitcast.13, f32[256]{0:T(256)S(1)} %compare_convert_fusion, f32[32,32]{1,0:T(8,128)S(1)} %broadcast_multiply_fusion, ...), kind=kLoop, calls=%fused_computation.133 | loop fusion | flops 17039360 | bytes 48419848 | tf_op jit(solution)/shard_map/add | solution.py:127
  327.0 2.4 multiply_add_fusion.1
  329.4 1.7 fusion.122
  331.1 1.7 fusion.121
  332.9 1.3 collective-permute-start.12
  334.2 5.0 %collective-permute-start.13 = (f32[4,32,256]{2,1,0:T(8,128)S(1)}, f32[4,32,256]{2,1,0:T(8,128)S(1)}, u32[]{:S(2)}, u32[]{:S(2)}) collective-permute-start(f32[4,32,256]{2,1,0:T(8,128)S(1)} %get-tuple-element.38), channel_id=1, source_target_pairs={{0,8},{8,16},{16,24},{1,9},{9,17},{17,25},{2,10},{10,18},{18,26},{... | collective-permute-start | bytes 393224 | tf_op jit(solution)/shard_map/ppermute | solution.py:29
  339.1 1.8 fusion.120
  340.9 0.7 collective-permute-done.13
  341.7 1.9 collective-permute-start.14
  343.6 4.1 %collective-permute-start.15 = (f32[40,4,256]{2,1,0:T(4,128)S(1)}, f32[40,4,256]{2,1,0:T(4,128)S(1)}, u32[]{:S(2)}, u32[]{:S(2)}) collective-permute-start(f32[40,4,256]{2,1,0:T(4,128)S(1)} %get-tuple-element.17), channel_id=1, source_target_pairs={{0,1},{1,2},{2,3},{3,4},{4,5},{5,6},{6,7},{8,9},{9,10},{10,11},{11... | collective-permute-start | bytes 491528 | tf_op jit(solution)/shard_map/ppermute | solution.py:29
  347.8 1.7 fusion.119
  349.5 3.5 collective-permute-done.15
  353.0 2.0 pad_maximum_fusion.3
  354.9 10.7 %add_bitcast_fusion = (f32[1,32,32,256]{3,2,1,0:T(8,128)}, f32[32,32,256]{2,1,0:T(8,128)S(1)}, f32[32,32,256]{2,1,0:T(8,128)}) fusion(f32[32,32,256]{2,1,0:T(8,128)S(1)} %multiply_add_fusion.3, f32[32,32,256]{2,1,0:T(8,128)S(1)} %multiply_add_fusion.1, s32[]{:T(128)S(6)} %min.6, bf16[512,32,256]{2,1,0:T(8,128)(2,1)S(1)} %bitcast.36, ...), kind=kLoop, calls=%fused_computation.204 | loop fusion | flops 15204352 | bytes 40026116 | tf_op jit(solution)/shard_map/broadcast_in_dim | solution.py:129
  365.6 4.1 %fusion.72 = f32[1,32,32,256]{3,2,1,0:T(8,128)} fusion(f32[32,32,256]{2,1,0:T(8,128)} %get-tuple-element.4, f32[32,32,256]{2,1,0:T(8,128)S(1)} %get-tuple-element.3, f32[32,32,256]{2,1,0:T(8,128)S(1)} %get-tuple-element.8, f32[32,32,256]{2,1,0:T(8,128)S(1)} %get-tuple-element.5, f32[]{:T(128)} %bitcast.14, f32[256]{0:T(256)S(1)} %compare_convert_fusion, ...), kind=kLoop, calls=%fused_computation.135 | loop fusion | flops 4718592 | bytes 30413832 | tf_op jit(solution)/shard_map/broadcast_in_dim | solution.py:129
  (38 shorter events, 0.4 us)
Async XLA Ops:
  7.2 151.3 %all-gather.3.cloned.1.call-start = ((), (), s32[]{:S(2)}) async-start(), calls=%async_computation.1 | async-start | bytes 8912896 | tf_op jit(solution)/shard_map/all_gather | solution.py:105
  7.9 223.0 %all-gather.5.cloned.1.call-start = ((), (), s32[]{:S(2)}) async-start(), calls=%async_computation.2 | async-start | bytes 8912896 | tf_op jit(solution)/shard_map/all_gather | solution.py:107
  14.0 7.2 %copy-start.1 = (f32[1,32,32,256]{3,2,1,0:T(8,128)S(1)}, f32[1,32,32,256]{3,2,1,0:T(8,128)}, u32[]{:S(2)}) copy-start(f32[1,32,32,256]{3,2,1,0:T(8,128)} %param.16) | copy-start | bytes 3145732
  14.0 13.1 %copy-start.5 = (s32[1,3]{1,0:T(1,128)S(1)}, s32[1,3]{1,0:T(1,128)}, u32[]{:S(2)}) copy-start(s32[1,3]{1,0:T(1,128)} %param.14) | copy-start | bytes 40
  14.0 15.0 %copy-start = (f32[1,32,32,256]{3,2,1,0:T(8,128)S(1)}, f32[1,32,32,256]{3,2,1,0:T(8,128)}, u32[]{:S(2)}) copy-start(f32[1,32,32,256]{3,2,1,0:T(8,128)} %param.18) | copy-start | bytes 3145732
  14.0 139.0 %all-to-all-start = ((bf16[16,32,32,256]{3,2,1,0:T(8,128)(2,1)}), bf16[16,32,32,256]{3,2,1,0:T(8,128)(2,1)}, u32[]{:S(2)}, u32[]{:S(2)}) async-start(bf16[16,32,32,256]{3,2,1,0:T(8,128)(2,1)} %stack.2), calls=%async_computation | async-start | bytes 16777216 | tf_op jit(solution)/shard_map/all_to_all | solution.py:16
  21.2 114.1 %collective-permute-start = (f32[4,32,256]{2,1,0:T(8,128)S(1)}, f32[4,32,256]{2,1,0:T(8,128)S(1)}, u32[]{:S(2)}, u32[]{:S(2)}) collective-permute-start(f32[4,32,256]{2,1,0:T(8,128)S(1)} %get-tuple-element.69), channel_id=1, source_target_pairs={{8,0},{16,8},{24,16},{9,1},{17,9},{25,17},{10,2},{18,10},{26,18},{... | collective-permute-start | bytes 393224 | tf_op jit(solution)/shard_map/ppermute | solution.py:32
  22.5 112.8 %collective-permute-start.1 = (f32[4,32,256]{2,1,0:T(8,128)S(1)}, f32[4,32,256]{2,1,0:T(8,128)S(1)}, u32[]{:S(2)}, u32[]{:S(2)}) collective-permute-start(f32[4,32,256]{2,1,0:T(8,128)S(1)} %get-tuple-element.68), channel_id=1, source_target_pairs={{0,8},{8,16},{16,24},{1,9},{9,17},{17,25},{2,10},{10,18},{18,26},{... | collective-permute-start | bytes 393224 | tf_op jit(solution)/shard_map/ppermute | solution.py:29
  35.8 108.0 %copy-start.6 = (s32[4]{0:T(128)S(1)}, s32[4]{0:T(128)}, u32[]{:S(2)}) copy-start(s32[4]{0:T(128)} %param.13) | copy-start | bytes 52
  35.8 109.2 %copy-start.4 = (f32[1,4]{1,0:T(1,128)S(1)}, f32[1,4]{1,0:T(1,128)}, u32[]{:S(2)}) copy-start(f32[1,4]{1,0:T(1,128)} %param.15) | copy-start | bytes 52
  135.4 10.2 %collective-permute-start.2 = (f32[40,4,256]{2,1,0:T(4,128)S(1)}, f32[40,4,256]{2,1,0:T(4,128)S(1)}, u32[]{:S(2)}, u32[]{:S(2)}) collective-permute-start(f32[40,4,256]{2,1,0:T(4,128)S(1)} %get-tuple-element.28), channel_id=1, source_target_pairs={{1,0},{2,1},{3,2},{4,3},{5,4},{6,5},{7,6},{9,8},{10,9},{11,10},{12... | collective-permute-start | bytes 491528 | tf_op jit(solution)/shard_map/ppermute | solution.py:32
  141.3 9.6 %collective-permute-start.3 = (f32[40,4,256]{2,1,0:T(4,128)S(1)}, f32[40,4,256]{2,1,0:T(4,128)S(1)}, u32[]{:S(2)}, u32[]{:S(2)}) collective-permute-start(f32[40,4,256]{2,1,0:T(4,128)S(1)} %get-tuple-element.29), channel_id=1, source_target_pairs={{0,1},{1,2},{2,3},{3,4},{4,5},{5,6},{6,7},{8,9},{9,10},{10,11},{11... | collective-permute-start | bytes 491528 | tf_op jit(solution)/shard_map/ppermute | solution.py:29
  230.9 12.5 %slice-start = ((s8[8388608]{0:T(1024)(128)(4,1)}), s8[4194304]{0:T(1024)(128)(4,1)S(1)}, s32[]{:S(2)}) async-start(s8[8388608]{0:T(1024)(128)(4,1)} %bitcast.35), calls=%async_computation.3 | async-start | bytes 8388608
  230.9 12.5 %slice-start.1 = ((s8[8388608]{0:T(1024)(128)(4,1)}), s8[4194304]{0:T(1024)(128)(4,1)S(1)}, s32[]{:S(2)}) async-start(s8[8388608]{0:T(1024)(128)(4,1)} %bitcast.35), calls=%async_computation.4 | async-start | bytes 8388608
  243.4 31.8 %copy-start.2 = (f32[32,32,256]{2,1,0:T(8,128)}, f32[32,32,256]{2,1,0:T(8,128)S(1)}, u32[]{:S(2)}) copy-start(f32[32,32,256]{2,1,0:T(8,128)S(1)} %get-tuple-element.11) | copy-start | bytes 3145732
  249.6 7.6 %collective-permute-start.4 = (f32[4,32,256]{2,1,0:T(8,128)S(1)}, f32[4,32,256]{2,1,0:T(8,128)S(1)}, u32[]{:S(2)}, u32[]{:S(2)}) collective-permute-start(f32[4,32,256]{2,1,0:T(8,128)S(1)} %get-tuple-element.59), channel_id=1, source_target_pairs={{8,0},{16,8},{24,16},{9,1},{17,9},{25,17},{10,2},{18,10},{26,18},{... | collective-permute-start | bytes 393224 | tf_op jit(solution)/shard_map/ppermute | solution.py:32
  250.9 7.4 %collective-permute-start.5 = (f32[4,32,256]{2,1,0:T(8,128)S(1)}, f32[4,32,256]{2,1,0:T(8,128)S(1)}, u32[]{:S(2)}, u32[]{:S(2)}) collective-permute-start(f32[4,32,256]{2,1,0:T(8,128)S(1)} %get-tuple-element.58), channel_id=1, source_target_pairs={{0,8},{8,16},{16,24},{1,9},{9,17},{17,25},{2,10},{10,18},{18,26},{... | collective-permute-start | bytes 393224 | tf_op jit(solution)/shard_map/ppermute | solution.py:29
  258.3 9.3 %collective-permute-start.6 = (f32[40,4,256]{2,1,0:T(4,128)S(1)}, f32[40,4,256]{2,1,0:T(4,128)S(1)}, u32[]{:S(2)}, u32[]{:S(2)}) collective-permute-start(f32[40,4,256]{2,1,0:T(4,128)S(1)} %get-tuple-element.24), channel_id=1, source_target_pairs={{1,0},{2,1},{3,2},{4,3},{5,4},{6,5},{7,6},{9,8},{10,9},{11,10},{12... | collective-permute-start | bytes 491528 | tf_op jit(solution)/shard_map/ppermute | solution.py:32
  263.9 9.3 %collective-permute-start.7 = (f32[40,4,256]{2,1,0:T(4,128)S(1)}, f32[40,4,256]{2,1,0:T(4,128)S(1)}, u32[]{:S(2)}, u32[]{:S(2)}) collective-permute-start(f32[40,4,256]{2,1,0:T(4,128)S(1)} %get-tuple-element.25), channel_id=1, source_target_pairs={{0,1},{1,2},{2,3},{3,4},{4,5},{5,6},{6,7},{8,9},{9,10},{10,11},{11... | collective-permute-start | bytes 491528 | tf_op jit(solution)/shard_map/ppermute | solution.py:29
  293.0 8.0 %collective-permute-start.8 = (f32[4,32,256]{2,1,0:T(8,128)S(1)}, f32[4,32,256]{2,1,0:T(8,128)S(1)}, u32[]{:S(2)}, u32[]{:S(2)}) collective-permute-start(f32[4,32,256]{2,1,0:T(8,128)S(1)} %get-tuple-element.49), channel_id=1, source_target_pairs={{8,0},{16,8},{24,16},{9,1},{17,9},{25,17},{10,2},{18,10},{26,18},{... | collective-permute-start | bytes 393224 | tf_op jit(solution)/shard_map/ppermute | solution.py:32
  294.3 7.5 %collective-permute-start.9 = (f32[4,32,256]{2,1,0:T(8,128)S(1)}, f32[4,32,256]{2,1,0:T(8,128)S(1)}, u32[]{:S(2)}, u32[]{:S(2)}) collective-permute-start(f32[4,32,256]{2,1,0:T(8,128)S(1)} %get-tuple-element.48), channel_id=1, source_target_pairs={{0,8},{8,16},{16,24},{1,9},{9,17},{17,25},{2,10},{10,18},{18,26},{... | collective-permute-start | bytes 393224 | tf_op jit(solution)/shard_map/ppermute | solution.py:29
  301.8 7.5 %collective-permute-start.10 = (f32[40,4,256]{2,1,0:T(4,128)S(1)}, f32[40,4,256]{2,1,0:T(4,128)S(1)}, u32[]{:S(2)}, u32[]{:S(2)}) collective-permute-start(f32[40,4,256]{2,1,0:T(4,128)S(1)} %get-tuple-element.20), channel_id=1, source_target_pairs={{1,0},{2,1},{3,2},{4,3},{5,4},{6,5},{7,6},{9,8},{10,9},{11,10},{12... | collective-permute-start | bytes 491528 | tf_op jit(solution)/shard_map/ppermute | solution.py:32
  303.7 9.3 %collective-permute-start.11 = (f32[40,4,256]{2,1,0:T(4,128)S(1)}, f32[40,4,256]{2,1,0:T(4,128)S(1)}, u32[]{:S(2)}, u32[]{:S(2)}) collective-permute-start(f32[40,4,256]{2,1,0:T(4,128)S(1)} %get-tuple-element.21), channel_id=1, source_target_pairs={{0,1},{1,2},{2,3},{3,4},{4,5},{5,6},{6,7},{8,9},{9,10},{10,11},{11... | collective-permute-start | bytes 491528 | tf_op jit(solution)/shard_map/ppermute | solution.py:29
  309.3 5.7 %copy-start.3 = (f32[32,32,256]{2,1,0:T(8,128)S(1)}, f32[32,32,256]{2,1,0:T(8,128)}, u32[]{:S(2)}) copy-start(f32[32,32,256]{2,1,0:T(8,128)} %copy-done.2) | copy-start | bytes 3145732
  332.9 8.0 %collective-permute-start.12 = (f32[4,32,256]{2,1,0:T(8,128)S(1)}, f32[4,32,256]{2,1,0:T(8,128)S(1)}, u32[]{:S(2)}, u32[]{:S(2)}) collective-permute-start(f32[4,32,256]{2,1,0:T(8,128)S(1)} %get-tuple-element.39), channel_id=1, source_target_pairs={{8,0},{16,8},{24,16},{9,1},{17,9},{25,17},{10,2},{18,10},{26,18},{... | collective-permute-start | bytes 393224 | tf_op jit(solution)/shard_map/ppermute | solution.py:32
  334.2 7.5 %collective-permute-start.13 = (f32[4,32,256]{2,1,0:T(8,128)S(1)}, f32[4,32,256]{2,1,0:T(8,128)S(1)}, u32[]{:S(2)}, u32[]{:S(2)}) collective-permute-start(f32[4,32,256]{2,1,0:T(8,128)S(1)} %get-tuple-element.38), channel_id=1, source_target_pairs={{0,8},{8,16},{16,24},{1,9},{9,17},{17,25},{2,10},{10,18},{18,26},{... | collective-permute-start | bytes 393224 | tf_op jit(solution)/shard_map/ppermute | solution.py:29
  341.7 7.8 %collective-permute-start.14 = (f32[40,4,256]{2,1,0:T(4,128)S(1)}, f32[40,4,256]{2,1,0:T(4,128)S(1)}, u32[]{:S(2)}, u32[]{:S(2)}) collective-permute-start(f32[40,4,256]{2,1,0:T(4,128)S(1)} %get-tuple-element.16), channel_id=1, source_target_pairs={{1,0},{2,1},{3,2},{4,3},{5,4},{6,5},{7,6},{9,8},{10,9},{11,10},{12... | collective-permute-start | bytes 491528 | tf_op jit(solution)/shard_map/ppermute | solution.py:32
  343.6 9.3 %collective-permute-start.15 = (f32[40,4,256]{2,1,0:T(4,128)S(1)}, f32[40,4,256]{2,1,0:T(4,128)S(1)}, u32[]{:S(2)}, u32[]{:S(2)}) collective-permute-start(f32[40,4,256]{2,1,0:T(4,128)S(1)} %get-tuple-element.17), channel_id=1, source_target_pairs={{0,1},{1,2},{2,3},{3,4},{4,5},{5,6},{6,7},{8,9},{9,10},{10,11},{11... | collective-permute-start | bytes 491528 | tf_op jit(solution)/shard_map/ppermute | solution.py:29
Sparse Core Ops, SparseCore 0:
  10.5 147.9 all-gather.2
  160.9 69.9 all-gather.4
